TPU v7x, 128 devices: a whole 4x4x4 slice. The times are simulated.
128 devices in a mesh: bx: 4 (over y), by: 4 (over x), bz: 8 (over z, core).
Axes of the slice: x: 4, y: 4, z: 4, core: 2. Of those that a mesh axis runs over, the one named last changes fastest.
Arguments:
- position: float32 [3, 128, 128, 2048], P(None, 'bx', 'by', 'bz'), may hold values from -2 to 2
- velocity: float32 [3, 128, 128, 2048], P(None, 'bx', 'by', 'bz'), may hold values from -3 to 3
- density: float32 [128, 128, 2048], P('bx', 'by', 'bz'), may hold values from 0.5 to 2
- energy: float32 [128, 128, 2048], P('bx', 'by', 'bz'), may hold values from 0.1 to 10
- pinned: int32 [128, 128, 2048], P('bx', 'by', 'bz'), may hold values 0 or 1
Outputs:
- velocity_new: float32 [3, 128, 128, 2048], P(None, 'bx', 'by', 'bz')
- accel: float32 [3, 128, 128, 2048], P(None, 'bx', 'by', 'bz')
- relaxed: float32 [3, 128, 128, 2048], P(None, 'bx', 'by', 'bz')
- density_new: float32 [128, 128, 2048], P('bx', 'by', 'bz')
- energy_new: float32 [128, 128, 2048], P('bx', 'by', 'bz')
All inputs are finite; a program needn't handle non-finite values. No bound on the sum of `pinned` on one device may be relied on, other than what follows from the above.
Results may differ from a plain program's by a relative error of at most 0.0003.
Values sent between devices are 32-bit elements; how exact they have to be, the bound alone decides.
A program may use at most 128 MiB of HBM per device.

v0:
```python
import jax
import jax.numpy as jnp
from jax import lax
from jax.sharding import PartitionSpec as P

CG_ITERS = 2
SWEEPS = 3
TIME_STEP = 0.6
RELAX_RATE = 0.8
CONSISTENT = 0.2


def from_behind(x, axis, by):
    length = lax.axis_size(axis)
    pairs = [(i, i + by) for i in range(length) if 0 <= i + by < length]
    return lax.ppermute(x, axis, pairs)


def padded(block, sides, width):
    for axis, dim in sides:
        count = lax.axis_size(axis)
        forward = [(i, i + 1) for i in range(count - 1)]
        backward = [(target, source) for source, target in forward]
        low = lax.ppermute(
            lax.slice_in_dim(block, block.shape[dim] - width, None, axis=dim), axis, forward
        )
        high = lax.ppermute(lax.slice_in_dim(block, 0, width, axis=dim), axis, backward)
        block = jnp.concatenate([low, block, high], axis=dim)
    return block


def shift_triple(along_dim, along, first, second):
    offsets = [0, 0, 0]
    offsets[along_dim] = along
    others = [d for d in range(3) if d != along_dim]
    offsets[others[0]] = first
    offsets[others[1]] = second
    return offsets


def select_at(extended, offsets):
    sizes = extended.shape[-3:]
    return extended[
        ...,
        1 + offsets[0] : sizes[0] - 1 + offsets[0],
        1 + offsets[1] : sizes[1] - 1 + offsets[1],
        1 + offsets[2] : sizes[2] - 1 + offsets[2],
    ]


def corner_force(pressure_ext):
    parts = []
    for along_dim in range(3):
        summed = 0.0
        for first in (0, -1):
            for second in (0, -1):
                summed = (
                    summed
                    + select_at(pressure_ext, shift_triple(along_dim, -1, first, second))
                    - select_at(pressure_ext, shift_triple(along_dim, 0, first, second))
                )
        parts.append(0.25 * summed)
    return jnp.stack(parts)


def node_mass(density_ext):
    summed = 0.0
    for first in (0, -1):
        for second in (0, -1):
            for third in (0, -1):
                summed = summed + select_at(density_ext, [first, second, third])
    return 0.125 * summed


def neighbours(extended):
    summed = 0.0
    for along_dim in range(3):
        for along in (-1, 1):
            summed = summed + select_at(extended, shift_triple(along_dim, along, 0, 0))
    return summed


def divergence(vel_ext):
    summed = 0.0
    for along_dim in range(3):
        for first in (0, 1):
            for second in (0, 1):
                summed = (
                    summed
                    + select_at(vel_ext[along_dim], shift_triple(along_dim, 1, first, second))
                    - select_at(vel_ext[along_dim], shift_triple(along_dim, 0, first, second))
                )
    return 0.25 * summed


def face_flux(packed, along_dim, along):
    speed = 0.0
    for first in (0, 1):
        for second in (0, 1):
            speed = speed + select_at(
                packed[along_dim], shift_triple(along_dim, along, first, second)
            )
    speed = 0.25 * speed
    upper = select_at(packed[3:5], shift_triple(along_dim, along, 0, 0))
    lower = select_at(packed[3:5], shift_triple(along_dim, along - 1, 0, 0))
    return speed * jnp.where(speed > 0, upper, lower)


def remap_cells(packed):
    result = select_at(packed[3:5], [0, 0, 0])
    for along_dim in range(3):
        result = result + face_flux(packed, along_dim, 1) - face_flux(packed, along_dim, 0)
    return result


def inner(first, second):
    return jnp.sum(first * second, axis=(1, 2, 3), keepdims=True)


def lower_cells(values):
    got = from_behind(values[..., -1:, :, :], "bx", 1)
    widened = jnp.concatenate([got, values], axis=-3)
    got = from_behind(widened[..., :, -1:, :], "by", 1)
    widened = jnp.concatenate([got, widened], axis=-2)
    got = from_behind(widened[..., :, :, -1:], "bz", 1)
    widened = jnp.concatenate([got, widened], axis=-1)
    return jnp.pad(widened, [(0, 0)] * (values.ndim - 3) + [(0, 1)] * 3)


def upper_nodes(values):
    got = from_behind(values[..., :1, :, :], "bx", -1)
    widened = jnp.concatenate([values, got], axis=-3)
    got = from_behind(widened[..., :, :1, :], "by", -1)
    widened = jnp.concatenate([widened, got], axis=-2)
    got = from_behind(widened[..., :, :, :1], "bz", -1)
    widened = jnp.concatenate([widened, got], axis=-1)
    return jnp.pad(widened, [(0, 0)] * (values.ndim - 3) + [(1, 0)] * 3)


def mass_apply(vector, masses):
    extended = padded(vector, (("bx", 1), ("by", 2), ("bz", 3)), 1)
    return masses * vector + CONSISTENT * (6.0 * vector + neighbours(extended))


def squares(residual):
    return lax.psum(inner(residual, residual), ("bx", "by", "bz"))


def one_sweep(relaxed, free):
    extended = padded(relaxed, (("bx", 1), ("by", 2), ("bz", 3)), 1)
    return relaxed + RELAX_RATE * free * (neighbours(extended) / 6.0 - relaxed)


def on_device(position, velocity, density, energy, pinned):
    cells = lower_cells(jnp.stack([density, energy]))
    force = corner_force(0.4 * cells[0] * cells[1])
    masses = node_mass(cells[0])
    solution = jnp.zeros_like(force)
    residual = force
    direction = force
    norm_now = squares(residual)
    for step_index in range(CG_ITERS):
        image = mass_apply(direction, masses)
        alpha = norm_now / lax.psum(inner(direction, image), ("bx", "by", "bz"))
        solution = solution + alpha * direction
        residual = residual - alpha * image
        norm_next = squares(residual)
        direction = residual + norm_next / norm_now * direction
        norm_now = norm_next
    velocity_new = velocity + TIME_STEP * solution
    vel_ext = upper_nodes(velocity_new)
    spread = divergence(vel_ext)
    pressure = 0.4 * density * energy
    energy_lag = energy - TIME_STEP * pressure * spread / density
    moved = position + TIME_STEP * velocity_new
    free = 1.0 - pinned.astype(jnp.float32)
    relaxed = moved
    for step_index in range(SWEEPS):
        relaxed = one_sweep(relaxed, free)
    packed = padded(
        jnp.concatenate([relaxed - moved, density[None], (density * energy_lag)[None]]),
        (("bx", 1), ("by", 2), ("bz", 3)),
        1,
    )
    remapped = remap_cells(packed)
    return (velocity_new, solution, relaxed, remapped[0], remapped[1])


def solution(mesh):
    in_specs = (
        P(None, "bx", "by", "bz"),
        P(None, "bx", "by", "bz"),
        P("bx", "by", "bz"),
        P("bx", "by", "bz"),
        P("bx", "by", "bz"),
    )
    out_specs = (
        P(None, "bx", "by", "bz"),
        P(None, "bx", "by", "bz"),
        P(None, "bx", "by", "bz"),
        P("bx", "by", "bz"),
        P("bx", "by", "bz"),
    )
    return jax.shard_map(
        on_device, mesh=mesh, in_specs=in_specs, out_specs=out_specs, check_vma=False
    )
```

profile of v0, /device:TPU:1, one launch (start us, length us, event | category | flops | bytes accessed | tf_op | source)
XLA Modules:
  0.0 638.1 jit_solution(13406718772434215634)
XLA Ops:
  1.6 4.0 collective-permute-start
  14.1 5.8 collective-permute-start.2
  29.0 4.0 collective-permute-start.3
  38.5 4.0 collective-permute-start.5
  45.3 4.1 collective-permute-done.6
  61.2 5.9 collective-permute-start.7
  67.1 7.7 %fusion.120 = f32[32,32,256]{2,1,0:T(8,128)} fusion(f32[34,34,258]{2,1,0:T(8,128)} %slice_bitcast_fusion.7), kind=kLoop, calls=%fused_computation.316 | loop fusion | flops 2097152 | bytes 9437184 | tf_op jit(solution)/shard_map/mul | solution.py:72
  80.7 16.0 %multiply_reduce_fusion.1 = (f32[3]{0:T(128)}, f32[3]{0:T(128)}, f32[3,32,32,256]{3,2,1,0:T(8,128)}) fusion(f32[1,32,32,256]{3,2,1,0:T(8,128)} %copy-done.4, f32[1,32,32,256]{3,2,1,0:T(8,128)S(1)} %multiply_bitcast_fusion.1, f32[1,32,32,256]{3,2,1,0:T(8,128)S(1)} %get-tuple-element.82, f32[3,34,34,1]{3,2,1,0:T(8,128)} %copy.67, ...), kind=kLoop, calls=%fused_computation.195 | loop fusion | flops 36175864 | bytes 7773304 | tf_op jit(solution)/shard_map/reduce_sum | solution.py:117
  96.7 64.6 %all-reduce.2 = (f32[3,1,1,1]{0,3,2,1:T(1,128)S(1)}, f32[3,1,1,1]{0,3,2,1:T(1,128)S(1)}) all-reduce(f32[3,1,1,1]{0,3,2,1:T(1,128)} %bitcast.58, f32[3,1,1,1]{0,3,2,1:T(1,128)} %bitcast.57), channel_id=1, replica_groups=mesh['bx'=4,'by'=4,'bz'=8] {'bx','by','bz'}, use_global_device_ids=true, to_apply=%region_1.2 | all-reduce | flops 6 | bytes 48 | tf_op jit(solution)/shard_map/psum | solution.py:146
  164.2 63.1 %psum.30 = f32[3,1,1,1]{0,3,2,1:T(1,128)S(1)} all-reduce(f32[3,1,1,1]{0,3,2,1:T(1,128)S(1)} %bitcast.60), channel_id=1, replica_groups=mesh['bx'=4,'by'=4,'bz'=8] {'bx','by','bz'}, use_global_device_ids=true, to_apply=%region_5.6 | all-reduce | flops 3 | bytes 24 | tf_op jit(solution)/shard_map/psum | solution.py:146
  251.8 5.8 collective-permute-start.13
  269.3 15.8 %fusion.67 = f32[3]{0:T(128)} fusion(f32[3,32,32,256]{3,2,1,0:T(8,128)} %copy-done.5, f32[3,34,34,1]{3,2,1,0:T(8,128)} %copy.71, f32[3,34,1,256]{3,2,1,0:T(1,128)S(1)} %collective-permute-done.12, f32[3,34,1,256]{3,2,1,0:T(1,128)S(1)} %collective-permute-done.11, f32[3,1,32,256]{3,2,1,0:T(8,128)S(1)} %collective-permute-done.10, ...), kind=kLoop, calls=%fused_computation.147 | loop fusion | flops 23592956 | bytes 4627564 | tf_op jit(solution)/shard_map/reduce_sum | solution.py:117
  285.1 63.9 %psum.31 = f32[3,1,1,1]{0,3,2,1:T(1,128)S(1)} all-reduce(f32[3,1,1,1]{0,3,2,1:T(1,128)} %bitcast.59), channel_id=1, replica_groups=mesh['bx'=4,'by'=4,'bz'=8] {'bx','by','bz'}, use_global_device_ids=true, to_apply=%region_7.8 | all-reduce | flops 3 | bytes 24 | tf_op jit(solution)/shard_map/psum | solution.py:164
  349.7 6.8 %multiply_add_fusion = (f32[3,32,32,256]{3,2,1,0:T(8,128)S(1)}, f32[3,32,32,256]{3,2,1,0:T(8,128)}, f32[3,32,32,256]{3,2,1,0:T(8,128)}) fusion(f32[3,32,32,256]{3,2,1,0:T(8,128)} %param.5, f32[3,32,32,256]{3,2,1,0:T(8,128)} %param.6, f32[3]{0:T(128)S(1)} %divide_bitcast_fusion, f32[1,32,32,256]{3,2,1,0:T(8,128)} %copy-done.4, ...), kind=kLoop, calls=%fused_computation.189 | loop fusion | flops 10223616 | bytes 22020132 | tf_op jit(solution)/shard_map/add | solution.py:175
  365.6 4.0 collective-permute-start.17
  378.9 5.4 collective-permute-start.20
  392.2 14.2 %fusion.57 = f32[3,32,32,256]{3,2,1,0:T(8,128)S(1)} fusion(f32[3,32,32,256]{3,2,1,0:T(8,128)} %copy-done.3, f32[3,34,34,1]{3,2,1,0:T(8,128)} %copy.81, f32[3,34,1,256]{3,2,1,0:T(1,128)S(1)} %copy.75, f32[3,34,1,256]{3,2,1,0:T(1,128)S(1)} %copy.73, f32[3,1,32,256]{3,2,1,0:T(8,128)S(1)} %collective-permute-done.16, ...), kind=kLoop, calls=%fused_computation.119 | loop fusion | flops 21233664 | bytes 7773280 | tf_op jit(solution)/shard_map/add | solution.py:151
  416.1 4.7 collective-permute-start.23
  422.2 4.3 collective-permute-done.34
  435.3 5.6 collective-permute-start.26
  462.1 14.5 %fusion.48 = f32[3,32,32,256]{3,2,1,0:T(8,128)S(1)} fusion(f32[3,32,32,256]{3,2,1,0:T(8,128)} %copy-done.6, f32[3,34,34,1]{3,2,1,0:T(8,128)} %copy.91, f32[3,34,1,256]{3,2,1,0:T(1,128)S(1)} %copy.85, f32[3,34,1,256]{3,2,1,0:T(1,128)S(1)} %copy.83, f32[3,1,32,256]{3,2,1,0:T(8,128)S(1)} %collective-permute-done.22, ...), kind=kLoop, calls=%fused_computation.92 | loop fusion | flops 21233664 | bytes 7773280 | tf_op jit(solution)/shard_map/add | solution.py:151
  481.2 4.7 select_maximum_fusion
  487.4 4.7 collective-permute-start.29
  510.0 20.4 %fusion.119 = f32[1,32,32,256]{3,2,1,0:T(8,128)} fusion(f32[32,32,256]{2,1,0:T(8,128)S(1)} %copy-done, f32[32,32,256]{2,1,0:T(8,128)} %param.8, f32[34,34,258]{2,1,0:T(8,128)} %get-tuple-element.39, f32[34,34,258]{2,1,0:T(8,128)} %get-tuple-element.38, f32[34,34,258]{2,1,0:T(8,128)S(1)} %get-tuple-element.37), kind=kLoop, calls=%fused_computation.292 | loop fusion | flops 8126464 | bytes 28311552 | tf_op jit(solution)/shard_map/broadcast_in_dim | solution.py:181
  536.4 16.5 %fusion.127 = (f32[3,32,32,256]{3,2,1,0:T(8,128)S(1)}, f32[3,32,32,256]{3,2,1,0:T(8,128)}) fusion(f32[3,32,32,256]{3,2,1,0:T(8,128)} %copy-done.3, f32[3,32,32,256]{3,2,1,0:T(8,128)} %copy-done.7, f32[3,34,34,1]{3,2,1,0:T(8,128)} %copy.101, f32[3,34,1,256]{3,2,1,0:T(1,128)S(1)} %copy.95, f32[3,1,32,256]{3,2,1,0:T(8,128)S(1)} %collective-permute-done.28, ...), kind=kLoop, calls=%fused_computation.365 | loop fusion | flops 22020096 | bytes 14064736 | tf_op jit(solution)/shard_map/sub | solution.py:181
  552.9 4.0 collective-permute-start.36
  560.8 4.1 collective-permute-done.37
  571.8 3.8 collective-permute-done.39
  577.2 3.9 fusion.130
  600.7 16.1 %pad_maximum_fusion = f32[5,34,34,258]{3,2,1,0:T(8,128)S(1)} fusion(f32[5,34,34,1]{3,2,1,0:T(8,128)} %copy.109, f32[5,34,1,256]{3,2,1,0:T(1,128)} %copy-done.19, f32[5,1,32,256]{3,2,1,0:T(8,128)S(1)} %collective-permute-done.37, f32[1,32,32,256]{3,2,1,0:T(8,128)} %fusion.119, f32[1,32,32,256]{3,2,1,0:T(8,128)} %bitcast.46, ...), kind=kLoop, calls=%fused_computation | loop fusion | flops 11929920 | bytes 11929920 | tf_op jit(solution)/shard_map/concatenate | solution.py:28
  621.0 6.0 broadcast_compare_fusion.1
  627.1 9.3 %fusion.84 = f32[2,32,32,256]{3,2,1,0:T(8,128)S(1)} fusion(f32[3,32,32,256]{3,2,1,0:T(8,128)S(1)} %get-tuple-element.26, f32[1,32,32,256]{3,2,1,0:T(8,128)S(1)} %bitcast.52, f32[5,34,34,1]{3,2,1,0:T(8,128)S(1)} %copy-done.13, f32[5,34,1,256]{3,2,1,0:T(1,128)S(1)} %copy-done.20, f32[5,34,1,256]{3,2,1,0:T(1,128)S(1)} %copy-done.18, ...), kind=kLoop, calls=%fused_computation.206 | loop fusion | flops 25690112 | bytes 15926432 | tf_op jit(solution)/shard_map/sub | solution.py:112
  (205 shorter events, 218.7 us)
Async XLA Ops:
  14.1 6.8 %collective-permute-start.2 = (f32[2,33,33,1]{2,0,3,1:T(2,128)S(1)}, f32[2,33,33,1]{2,0,3,1:T(2,128)}, u32[]{:S(2)}, u32[]{:S(2)}) collective-permute-start(f32[2,33,33,1]{2,0,3,1:T(2,128)S(1)} %copy.62), channel_id=1, source_target_pairs={{0,1},{1,2},{2,3},{3,4},{4,5},{5,6},{6,7},{8,9},{9,10},{10,11},{11... | collective-permute-start | bytes 26144 | tf_op jit(solution)/shard_map/ppermute | solution.py:16
  29.0 5.6 collective-permute-start.3
  38.5 6.8 %collective-permute-start.5 = (f32[3,34,1,256]{3,2,1,0:T(1,128)S(1)}, f32[3,34,1,256]{3,2,1,0:T(1,128)S(1)}, u32[]{:S(2)}, u32[]{:S(2)}) collective-permute-start(f32[3,34,1,256]{3,2,1,0:T(1,128)S(1)} %get-tuple-element.62), channel_id=1, source_target_pairs={{0,8},{8,16},{16,24},{1,9},{9,17},{17,25},{2,10},{10,18},{18,26},{... | collective-permute-start | bytes 313352 | tf_op jit(solution)/shard_map/ppermute | solution.py:24
  42.5 6.8 %collective-permute-start.6 = (f32[3,34,1,256]{3,2,1,0:T(1,128)S(1)}, f32[3,34,1,256]{3,2,1,0:T(1,128)S(1)}, u32[]{:S(2)}, u32[]{:S(2)}) collective-permute-start(f32[3,34,1,256]{3,2,1,0:T(1,128)S(1)} %get-tuple-element.63), channel_id=1, source_target_pairs={{8,0},{16,8},{24,16},{9,1},{17,9},{25,17},{10,2},{18,10},{26,18},{... | collective-permute-start | bytes 313352 | tf_op jit(solution)/shard_map/ppermute | solution.py:27
  58.9 18.8 %collective-permute-start.8 = (f32[3,34,34,1]{2,3,1,0:T(1,128)}, f32[3,34,34,1]{2,3,1,0:T(1,128)}, u32[]{:S(2)}, u32[]{:S(2)}) collective-permute-start(f32[3,34,34,1]{2,3,1,0:T(1,128)} %copy.66), channel_id=1, source_target_pairs={{1,0},{2,1},{3,2},{4,3},{5,4},{6,5},{7,6},{9,8},{10,9},{11,10},{12... | collective-permute-start | bytes 41624 | tf_op jit(solution)/shard_map/ppermute | solution.py:27
  61.2 13.6 %collective-permute-start.7 = (f32[3,34,34,1]{2,3,1,0:T(1,128)}, f32[3,34,34,1]{2,3,1,0:T(1,128)}, u32[]{:S(2)}, u32[]{:S(2)}) collective-permute-start(f32[3,34,34,1]{2,3,1,0:T(1,128)} %copy.64), channel_id=1, source_target_pairs={{0,1},{1,2},{2,3},{3,4},{4,5},{5,6},{6,7},{8,9},{9,10},{10,11},{11... | collective-permute-start | bytes 41624 | tf_op jit(solution)/shard_map/ppermute | solution.py:24
  240.0 5.4 collective-permute-start.12
  251.8 10.9 %collective-permute-start.13 = (f32[3,34,34,1]{2,3,1,0:T(1,128)}, f32[3,34,34,1]{2,3,1,0:T(1,128)}, u32[]{:S(2)}, u32[]{:S(2)}) collective-permute-start(f32[3,34,34,1]{2,3,1,0:T(1,128)} %copy.68), channel_id=1, source_target_pairs={{0,1},{1,2},{2,3},{3,4},{4,5},{5,6},{6,7},{8,9},{9,10},{10,11},{11... | collective-permute-start | bytes 41624 | tf_op jit(solution)/shard_map/ppermute | solution.py:24
  260.6 5.7 collective-permute-start.14
  364.2 5.6 collective-permute-start.18
  365.6 5.8 collective-permute-start.17
  378.9 11.1 %collective-permute-start.20 = (f32[3,34,34,1]{2,1,3,0:T(8,128)}, f32[3,34,34,1]{2,1,3,0:T(8,128)S(1)}, u32[]{:S(2)}, u32[]{:S(2)}) collective-permute-start(f32[3,34,34,1]{2,1,3,0:T(8,128)} %copy.80), channel_id=1, source_target_pairs={{1,0},{2,1},{3,2},{4,3},{5,4},{6,5},{7,6},{9,8},{10,9},{11,10},{12... | collective-permute-start | bytes 41624 | tf_op jit(solution)/shard_map/ppermute | solution.py:27
  406.4 5.5 collective-permute-start.21
  410.6 10.2 %collective-permute-start.33 = (f32[3,1,32,256]{3,2,1,0:T(8,128)S(1)}, f32[3,1,32,256]{3,2,1,0:T(8,128)S(1)}, u32[]{:S(2)}, u32[]{:S(2)}) collective-permute-start(f32[3,1,32,256]{3,2,1,0:T(8,128)S(1)} %slice.782), channel_id=1, source_target_pairs={{32,0},{64,32},{96,64},{33,1},{65,33},{97,65},{34,2},{66,34},{98,6... | collective-permute-start | bytes 294920 | tf_op jit(solution)/shard_map/ppermute | solution.py:16
  414.8 11.8 %collective-permute-start.24 = (f32[3,34,1,256]{3,1,2,0:T(8,128)S(1)}, f32[3,34,1,256]{3,1,2,0:T(8,128)S(1)}, u32[]{:S(2)}, u32[]{:S(2)}) collective-permute-start(f32[3,34,1,256]{3,1,2,0:T(8,128)S(1)} %copy.84), channel_id=1, source_target_pairs={{8,0},{16,8},{24,16},{9,1},{17,9},{25,17},{10,2},{18,10},{26,18},{... | collective-permute-start | bytes 313352 | tf_op jit(solution)/shard_map/ppermute | solution.py:27
  416.1 10.7 %collective-permute-start.23 = (f32[3,34,1,256]{3,1,2,0:T(8,128)S(1)}, f32[3,34,1,256]{3,1,2,0:T(8,128)S(1)}, u32[]{:S(2)}, u32[]{:S(2)}) collective-permute-start(f32[3,34,1,256]{3,1,2,0:T(8,128)S(1)} %copy.82), channel_id=1, source_target_pairs={{0,8},{8,16},{16,24},{1,9},{9,17},{17,25},{2,10},{10,18},{18,26},{... | collective-permute-start | bytes 313352 | tf_op jit(solution)/shard_map/ppermute | solution.py:24
  420.9 5.6 collective-permute-start.34
  435.3 24.7 %collective-permute-start.26 = (f32[3,34,34,1]{2,1,3,0:T(8,128)S(1)}, f32[3,34,34,1]{2,1,3,0:T(8,128)S(1)}, u32[]{:S(2)}, u32[]{:S(2)}) collective-permute-start(f32[3,34,34,1]{2,1,3,0:T(8,128)S(1)} %copy.90), channel_id=1, source_target_pairs={{1,0},{2,1},{3,2},{4,3},{5,4},{6,5},{7,6},{9,8},{10,9},{11,10},{12... | collective-permute-start | bytes 41624 | tf_op jit(solution)/shard_map/ppermute | solution.py:27
  440.9 16.8 %collective-permute-start.25 = (f32[3,34,34,1]{2,1,3,0:T(8,128)S(1)}, f32[3,34,34,1]{2,1,3,0:T(8,128)S(1)}, u32[]{:S(2)}, u32[]{:S(2)}) collective-permute-start(f32[3,34,34,1]{2,1,3,0:T(8,128)S(1)} %copy.88), channel_id=1, source_target_pairs={{0,1},{1,2},{2,3},{3,4},{4,5},{5,6},{6,7},{8,9},{9,10},{10,11},{11... | collective-permute-start | bytes 41624 | tf_op jit(solution)/shard_map/ppermute | solution.py:24
  450.0 5.5 collective-permute-start.35
  476.6 9.3 %collective-permute-start.27 = (f32[3,1,32,256]{3,2,1,0:T(8,128)S(1)}, f32[3,1,32,256]{3,2,1,0:T(8,128)S(1)}, u32[]{:S(2)}, u32[]{:S(2)}) collective-permute-start(f32[3,1,32,256]{3,2,1,0:T(8,128)S(1)} %get-tuple-element.64), channel_id=1, source_target_pairs={{0,32},{32,64},{64,96},{1,33},{33,65},{65,97},{2,34},{34,66},{66,9... | collective-permute-start | bytes 294920 | tf_op jit(solution)/shard_map/ppermute | solution.py:24
  479.9 6.0 collective-permute-start.28
  486.1 8.4 %collective-permute-start.30 = (f32[3,34,1,256]{3,1,2,0:T(8,128)S(1)}, f32[3,34,1,256]{3,1,2,0:T(8,128)S(1)}, u32[]{:S(2)}, u32[]{:S(2)}) collective-permute-start(f32[3,34,1,256]{3,1,2,0:T(8,128)S(1)} %copy.94), channel_id=1, source_target_pairs={{8,0},{16,8},{24,16},{9,1},{17,9},{25,17},{10,2},{18,10},{26,18},{... | collective-permute-start | bytes 313352 | tf_op jit(solution)/shard_map/ppermute | solution.py:27
  487.4 7.2 %collective-permute-start.29 = (f32[3,34,1,256]{3,1,2,0:T(8,128)S(1)}, f32[3,34,1,256]{3,1,2,0:T(8,128)S(1)}, u32[]{:S(2)}, u32[]{:S(2)}) collective-permute-start(f32[3,34,1,256]{3,1,2,0:T(8,128)S(1)} %copy.92), channel_id=1, source_target_pairs={{0,8},{8,16},{16,24},{1,9},{9,17},{17,25},{2,10},{10,18},{18,26},{... | collective-permute-start | bytes 313352 | tf_op jit(solution)/shard_map/ppermute | solution.py:24
  504.5 29.0 %collective-permute-start.32 = (f32[3,34,34,1]{2,1,3,0:T(8,128)}, f32[3,34,34,1]{2,1,3,0:T(8,128)}, u32[]{:S(2)}, u32[]{:S(2)}) collective-permute-start(f32[3,34,34,1]{2,1,3,0:T(8,128)} %copy.100), channel_id=1, source_target_pairs={{1,0},{2,1},{3,2},{4,3},{5,4},{6,5},{7,6},{9,8},{10,9},{11,10},{12... | collective-permute-start | bytes 41624 | tf_op jit(solution)/shard_map/ppermute | solution.py:27
  506.4 24.0 %collective-permute-start.31 = (f32[3,34,34,1]{2,1,3,0:T(8,128)}, f32[3,34,34,1]{2,1,3,0:T(8,128)}, u32[]{:S(2)}, u32[]{:S(2)}) collective-permute-start(f32[3,34,34,1]{2,1,3,0:T(8,128)} %copy.98), channel_id=1, source_target_pairs={{0,1},{1,2},{2,3},{3,4},{4,5},{5,6},{6,7},{8,9},{9,10},{10,11},{11... | collective-permute-start | bytes 41624 | tf_op jit(solution)/shard_map/ppermute | solution.py:24
  552.9 7.9 %collective-permute-start.36 = (f32[5,1,32,256]{3,2,1,0:T(8,128)S(1)}, f32[5,1,32,256]{3,2,1,0:T(8,128)S(1)}, u32[]{:S(2)}, u32[]{:S(2)}) collective-permute-start(f32[5,1,32,256]{3,2,1,0:T(8,128)S(1)} %get-tuple-element.42), channel_id=1, source_target_pairs={{0,32},{32,64},{64,96},{1,33},{33,65},{65,97},{2,34},{34,66},{66,9... | collective-permute-start | bytes 491528 | tf_op jit(solution)/shard_map/ppermute | solution.py:24
  556.9 8.0 %collective-permute-start.37 = (f32[5,1,32,256]{3,2,1,0:T(8,128)S(1)}, f32[5,1,32,256]{3,2,1,0:T(8,128)S(1)}, u32[]{:S(2)}, u32[]{:S(2)}) collective-permute-start(f32[5,1,32,256]{3,2,1,0:T(8,128)S(1)} %get-tuple-element.43), channel_id=1, source_target_pairs={{32,0},{64,32},{96,64},{33,1},{65,33},{97,65},{34,2},{66,34},{98,6... | collective-permute-start | bytes 491528 | tf_op jit(solution)/shard_map/ppermute | solution.py:27
  565.2 6.6 %collective-permute-start.38 = (f32[5,34,1,256]{3,2,1,0:T(1,128)S(1)}, f32[5,34,1,256]{3,2,1,0:T(1,128)S(1)}, u32[]{:S(2)}, u32[]{:S(2)}) collective-permute-start(f32[5,34,1,256]{3,2,1,0:T(1,128)S(1)} %get-tuple-element.40), channel_id=1, source_target_pairs={{0,8},{8,16},{16,24},{1,9},{9,17},{17,25},{2,10},{10,18},{18,26},{... | collective-permute-start | bytes 522248 | tf_op jit(solution)/shard_map/ppermute | solution.py:24
  568.5 7.1 %collective-permute-start.39 = (f32[5,34,1,256]{3,2,1,0:T(1,128)S(1)}, f32[5,34,1,256]{3,2,1,0:T(1,128)S(1)}, u32[]{:S(2)}, u32[]{:S(2)}) collective-permute-start(f32[5,34,1,256]{3,2,1,0:T(1,128)S(1)} %get-tuple-element.41), channel_id=1, source_target_pairs={{8,0},{16,8},{24,16},{9,1},{17,9},{25,17},{10,2},{18,10},{26,18},{... | collective-permute-start | bytes 522248 | tf_op jit(solution)/shard_map/ppermute | solution.py:27
  584.5 9.2 %collective-permute-start.41 = (f32[5,34,34,1]{2,3,1,0:T(1,128)}, f32[5,34,34,1]{2,3,1,0:T(1,128)}, u32[]{:S(2)}, u32[]{:S(2)}) collective-permute-start(f32[5,34,34,1]{2,3,1,0:T(1,128)} %copy.107), channel_id=1, source_target_pairs={{1,0},{2,1},{3,2},{4,3},{5,4},{6,5},{7,6},{9,8},{10,9},{11,10},{12... | collective-permute-start | bytes 69368 | tf_op jit(solution)/shard_map/ppermute | solution.py:27
  591.6 5.6 collective-permute-start.40
  (35 other events, 444.4 us)
where the time goes:
time: 647 us; the launch traced here: 638 us
  blocking collectives  192 us (30%)
  other arithmetic  178 us (28%)
  starting transfers between devices  118 us (18%)
  local copies, waits for them, and re-layouts  98.8 us (15%)
  waiting for transfers between devices  49.5 us (8%)
    psum x2, blocking collectives, squares(): return lax.psum(inner(residual, residual), ('bx', 'by', 'bz'))  128 us
    ppermute x18, starting transfers between devices, padded(): lax.ppermute(lax.slice_in_dim(block, block.shape[dim] - width, None, axis...  64.5 us
    psum x1, blocking collectives, on_device(): alpha = norm_now / lax.psum(inner(direction, image), ('bx', 'by', 'bz'))  63.9 us
    ppermute x18, starting transfers between devices, padded(): lax.ppermute(lax.slice_in_dim(block, 0, width, axis=dim), axis, backward)  36.5 us
    reduce_sum x3, other arithmetic, inner(): return jnp.sum(first * second, axis=(1, 2, 3), keepdims=True)  34.7 us
    slice x19, local copies, waits for them, and re-layouts, padded(): lax.slice_in_dim(block, block.shape[dim] - width, None, axis=dim)  30.9 us
    ppermute x18, waiting for transfers between devices, padded(): lax.ppermute(lax.slice_in_dim(block, 0, width, axis=dim), axis, backward)  30.7 us
    add x2, other arithmetic, one_sweep(): return relaxed + RELAX_RATE * free * (neighbours(extended) / 6.0 - relaxed)  28.6 us
  transfers between devices with their start and end apart: 42, of which 22 were waited for; matrix products, arithmetic and copies ran while one was open for 11% of the time, Pallas kernels for 0%

commit v1 on v0

--- a/solution.py
+++ b/solution.py
@@ -2,6 +2,7 @@
 import jax.numpy as jnp
 from jax import lax
 from jax.sharding import PartitionSpec as P
+from jax.lax import psum
 
 CG_ITERS = 2
 SWEEPS = 3
@@ -143,7 +144,10 @@
 
 
 def squares(residual):
-    return lax.psum(inner(residual, residual), ("bx", "by", "bz"))
+    change_views_all = lambda load, across, named_axis: psum(
+        psum(load, axis_name=across), named_axis
+    )
+    return change_views_all(inner(residual, residual), ("by", "bz"), "bx")
 
 
 def one_sweep(relaxed, free):

time: 647 us -> 726 us (1.12)
  blocking collectives: 192 us -> 268 us
    psum x1 -> x2, blocking collectives: 63.9 us -> 128 us  [on_device(): alpha = norm_now / lax.psum(inner(direction, image), ('bx', 'by', 'bz'))]
    psum x2 -> x4, blocking collectives: 128 us -> 139 us  [the longest x2 126 us: squares(): psum(load, axis_name=across)]
  transfers between devices with their start and end apart: 42 -> 42, of which waited for: 22 -> 21; matrix products, arithmetic and copies ran while one was open for 11% -> 10% of each run, Pallas kernels for 0% -> 0%
where the time goes in v1:
time: 726 us; the launch traced here: 717 us
  blocking collectives  268 us (37%)
  other arithmetic  178 us (25%)
  starting transfers between devices  120 us (17%)
  local copies, waits for them, and re-layouts  98.9 us (14%)
  waiting for transfers between devices  49.6 us (7%)
    psum x2, blocking collectives, on_device(): alpha = norm_now / lax.psum(inner(direction, image), ('bx', 'by', 'bz'))  128 us
    psum x2, blocking collectives, squares(): psum(load, axis_name=across)  126 us
    ppermute x18, starting transfers between devices, padded(): lax.ppermute(lax.slice_in_dim(block, block.shape[dim] - width, None, axis...  63.7 us
    ppermute x18, starting transfers between devices, padded(): lax.ppermute(lax.slice_in_dim(block, 0, width, axis=dim), axis, backward)  39.3 us
    reduce_sum x3, other arithmetic, inner(): return jnp.sum(first * second, axis=(1, 2, 3), keepdims=True)  34.8 us
    slice x19, local copies, waits for them, and re-layouts, padded(): lax.slice_in_dim(block, block.shape[dim] - width, None, axis=dim)  30.9 us
    ppermute x18, waiting for transfers between devices, padded(): lax.ppermute(lax.slice_in_dim(block, 0, width, axis=dim), axis, backward)  30.7 us
    add x2, other arithmetic, one_sweep(): return relaxed + RELAX_RATE * free * (neighbours(extended) / 6.0 - relaxed)  29 us
  transfers between devices with their start and end apart: 42, of which 21 were waited for; matrix products, arithmetic and copies ran while one was open for 10% of the time, Pallas kernels for 0%

profile of v1, /device:TPU:1, one launch (start us, length us, event | category | flops | bytes accessed | tf_op | source)
XLA Modules:
  0.0 716.7 jit_solution(15859905743366558238)
XLA Ops:
  1.6 4.0 collective-permute-start
  14.1 5.8 collective-permute-start.2
  45.3 4.1 collective-permute-done.6
  61.2 5.9 collective-permute-start.7
  67.1 7.7 %fusion.120 = f32[32,32,256]{2,1,0:T(8,128)} fusion(f32[34,34,258]{2,1,0:T(8,128)} %slice_bitcast_fusion.7), kind=kLoop, calls=%fused_computation.316 | loop fusion | flops 2097152 | bytes 9437184 | tf_op jit(solution)/shard_map/mul | solution.py:73
  80.7 16.0 %multiply_reduce_fusion.1 = (f32[3]{0:T(128)}, f32[3]{0:T(128)}, f32[3,32,32,256]{3,2,1,0:T(8,128)}) fusion(f32[1,32,32,256]{3,2,1,0:T(8,128)} %copy-done.4, f32[1,32,32,256]{3,2,1,0:T(8,128)S(1)} %multiply_bitcast_fusion.1, f32[1,32,32,256]{3,2,1,0:T(8,128)S(1)} %get-tuple-element.80, f32[3,34,34,1]{3,2,1,0:T(8,128)} %copy.67, ...), kind=kLoop, calls=%fused_computation.195 | loop fusion | flops 36175864 | bytes 7773304 | tf_op jit(solution)/shard_map/reduce_sum | solution.py:118
  96.7 61.0 %psum.42 = f32[3,1,1,1]{0,3,2,1:T(1,128)S(1)} all-reduce(f32[3,1,1,1]{0,3,2,1:T(1,128)} %bitcast.58), channel_id=1, replica_groups=mesh['bx'=4,'by'=4,'bz'=8] {'by','bz'}, use_global_device_ids=true, to_apply=%region_1.2 | all-reduce | flops 3 | bytes 24 | tf_op jit(solution)/shard_map/psum | solution.py:148
  157.7 66.5 %psum.44 = f32[3,1,1,1]{0,3,2,1:T(1,128)S(1)} all-reduce(f32[3,1,1,1]{0,3,2,1:T(1,128)} %bitcast.57), channel_id=1, replica_groups=mesh['bx'=4,'by'=4,'bz'=8] {'bx','by','bz'}, use_global_device_ids=true, to_apply=%region_4.5 | all-reduce | flops 3 | bytes 24 | tf_op jit(solution)/shard_map/psum | solution.py:168
  224.2 6.7 psum.43
  233.8 64.9 %psum.45 = f32[3,1,1,1]{0,3,2,1:T(1,128)S(1)} all-reduce(f32[3,1,1,1]{0,3,2,1:T(1,128)S(1)} %bitcast.60), channel_id=1, replica_groups=mesh['bx'=4,'by'=4,'bz'=8] {'by','bz'}, use_global_device_ids=true, to_apply=%region_6.7 | all-reduce | flops 3 | bytes 24 | tf_op jit(solution)/shard_map/psum | solution.py:148
  298.7 6.6 psum.46
  336.1 6.0 collective-permute-start.14
  348.0 15.8 %fusion.67 = f32[3]{0:T(128)} fusion(f32[3,32,32,256]{3,2,1,0:T(8,128)} %copy-done.5, f32[3,34,34,1]{3,2,1,0:T(8,128)} %copy.71, f32[3,34,1,256]{3,2,1,0:T(1,128)S(1)} %collective-permute-done.12, f32[3,34,1,256]{3,2,1,0:T(1,128)S(1)} %collective-permute-done.11, f32[3,1,32,256]{3,2,1,0:T(8,128)S(1)} %collective-permute-done.10, ...), kind=kLoop, calls=%fused_computation.147 | loop fusion | flops 23592956 | bytes 4627564 | tf_op jit(solution)/shard_map/reduce_sum | solution.py:118
  363.9 61.9 %psum.47 = f32[3,1,1,1]{0,3,2,1:T(1,128)S(1)} all-reduce(f32[3,1,1,1]{0,3,2,1:T(1,128)} %bitcast.59), channel_id=1, replica_groups=mesh['bx'=4,'by'=4,'bz'=8] {'bx','by','bz'}, use_global_device_ids=true, to_apply=%region_9.10 | all-reduce | flops 3 | bytes 24 | tf_op jit(solution)/shard_map/psum | solution.py:168
  426.4 6.8 multiply_add_fusion
  443.0 4.0 collective-permute-start.17
  456.4 5.5 collective-permute-start.20
  469.8 14.2 %fusion.57 = f32[3,32,32,256]{3,2,1,0:T(8,128)S(1)} fusion(f32[3,32,32,256]{3,2,1,0:T(8,128)} %copy-done.3, f32[3,34,34,1]{3,2,1,0:T(8,128)} %copy.81, f32[3,34,1,256]{3,2,1,0:T(1,128)S(1)} %copy.75, f32[3,34,1,256]{3,2,1,0:T(1,128)S(1)} %copy.73, f32[3,1,32,256]{3,2,1,0:T(8,128)S(1)} %collective-permute-done.16, ...), kind=kLoop, calls=%fused_computation.119 | loop fusion | flops 21233664 | bytes 7773280 | tf_op jit(solution)/shard_map/add | solution.py:155
  493.9 4.7 collective-permute-start.23
  500.0 4.3 collective-permute-done.34
  513.1 4.5 collective-permute-start.26
  517.6 4.0 collective-permute-start.25
  539.1 14.9 %fusion.48 = f32[3,32,32,256]{3,2,1,0:T(8,128)S(1)} fusion(f32[3,32,32,256]{3,2,1,0:T(8,128)} %copy-done.6, f32[3,34,34,1]{3,2,1,0:T(8,128)} %copy.91, f32[3,34,1,256]{3,2,1,0:T(1,128)S(1)} %copy.85, f32[3,34,1,256]{3,2,1,0:T(1,128)S(1)} %copy.83, f32[3,1,32,256]{3,2,1,0:T(8,128)S(1)} %collective-permute-done.22, ...), kind=kLoop, calls=%fused_computation.92 | loop fusion | flops 21233664 | bytes 7773280 | tf_op jit(solution)/shard_map/add | solution.py:155
  558.2 4.7 select_maximum_fusion
  564.5 4.7 collective-permute-start.29
  587.0 20.1 %fusion.119 = f32[1,32,32,256]{3,2,1,0:T(8,128)} fusion(f32[32,32,256]{2,1,0:T(8,128)S(1)} %copy-done, f32[32,32,256]{2,1,0:T(8,128)} %param.8, f32[34,34,258]{2,1,0:T(8,128)} %get-tuple-element.37, f32[34,34,258]{2,1,0:T(8,128)} %get-tuple-element.36, f32[34,34,258]{2,1,0:T(8,128)S(1)} %get-tuple-element.35), kind=kLoop, calls=%fused_computation.292 | loop fusion | flops 8126464 | bytes 28311552 | tf_op jit(solution)/shard_map/broadcast_in_dim | solution.py:185
  613.2 16.4 %fusion.127 = (f32[3,32,32,256]{3,2,1,0:T(8,128)S(1)}, f32[3,32,32,256]{3,2,1,0:T(8,128)}) fusion(f32[3,32,32,256]{3,2,1,0:T(8,128)} %copy-done.3, f32[3,32,32,256]{3,2,1,0:T(8,128)} %copy-done.7, f32[3,34,34,1]{3,2,1,0:T(8,128)} %copy.101, f32[3,34,1,256]{3,2,1,0:T(1,128)S(1)} %copy.95, f32[3,1,32,256]{3,2,1,0:T(8,128)S(1)} %collective-permute-done.28, ...), kind=kLoop, calls=%fused_computation.365 | loop fusion | flops 22020096 | bytes 14064736 | tf_op jit(solution)/shard_map/sub | solution.py:185
  629.6 4.0 collective-permute-start.36
  637.5 4.1 collective-permute-done.37
  679.3 16.1 %pad_maximum_fusion = f32[5,34,34,258]{3,2,1,0:T(8,128)S(1)} fusion(f32[5,34,34,1]{3,2,1,0:T(8,128)} %copy.109, f32[5,34,1,256]{3,2,1,0:T(1,128)} %copy-done.19, f32[5,1,32,256]{3,2,1,0:T(8,128)S(1)} %collective-permute-done.37, f32[1,32,32,256]{3,2,1,0:T(8,128)} %fusion.119, f32[1,32,32,256]{3,2,1,0:T(8,128)} %bitcast.46, ...), kind=kLoop, calls=%fused_computation | loop fusion | flops 11929920 | bytes 11929920 | tf_op jit(solution)/shard_map/concatenate | solution.py:29
  699.6 6.0 broadcast_compare_fusion.1
  705.7 9.3 %fusion.84 = f32[2,32,32,256]{3,2,1,0:T(8,128)S(1)} fusion(f32[3,32,32,256]{3,2,1,0:T(8,128)S(1)} %get-tuple-element.24, f32[1,32,32,256]{3,2,1,0:T(8,128)S(1)} %bitcast.52, f32[5,34,34,1]{3,2,1,0:T(8,128)S(1)} %copy-done.13, f32[5,34,1,256]{3,2,1,0:T(1,128)S(1)} %copy-done.20, f32[5,34,1,256]{3,2,1,0:T(1,128)S(1)} %copy-done.18, ...), kind=kLoop, calls=%fused_computation.206 | loop fusion | flops 25690112 | bytes 15926432 | tf_op jit(solution)/shard_map/sub | solution.py:113
  (208 shorter events, 233.5 us)
Async XLA Ops:
  14.1 6.8 collective-permute-start.2
  29.0 5.6 collective-permute-start.3
  38.5 6.8 collective-permute-start.5
  42.5 6.8 collective-permute-start.6
  58.9 18.8 %collective-permute-start.8 = (f32[3,34,34,1]{2,3,1,0:T(1,128)}, f32[3,34,34,1]{2,3,1,0:T(1,128)}, u32[]{:S(2)}, u32[]{:S(2)}) collective-permute-start(f32[3,34,34,1]{2,3,1,0:T(1,128)} %copy.66), channel_id=1, source_target_pairs={{1,0},{2,1},{3,2},{4,3},{5,4},{6,5},{7,6},{9,8},{10,9},{11,10},{12... | collective-permute-start | bytes 41624 | tf_op jit(solution)/shard_map/ppermute | solution.py:28
  61.2 13.6 %collective-permute-start.7 = (f32[3,34,34,1]{2,3,1,0:T(1,128)}, f32[3,34,34,1]{2,3,1,0:T(1,128)}, u32[]{:S(2)}, u32[]{:S(2)}) collective-permute-start(f32[3,34,34,1]{2,3,1,0:T(1,128)} %copy.64), channel_id=1, source_target_pairs={{0,1},{1,2},{2,3},{3,4},{4,5},{5,6},{6,7},{8,9},{9,10},{10,11},{11... | collective-permute-start | bytes 41624 | tf_op jit(solution)/shard_map/ppermute | solution.py:25
  318.1 5.4 collective-permute-start.12
  329.9 12.2 %collective-permute-start.13 = (f32[3,34,34,1]{2,3,1,0:T(1,128)}, f32[3,34,34,1]{2,3,1,0:T(1,128)}, u32[]{:S(2)}, u32[]{:S(2)}) collective-permute-start(f32[3,34,34,1]{2,3,1,0:T(1,128)} %copy.68), channel_id=1, source_target_pairs={{0,1},{1,2},{2,3},{3,4},{4,5},{5,6},{6,7},{8,9},{9,10},{10,11},{11... | collective-permute-start | bytes 41624 | tf_op jit(solution)/shard_map/ppermute | solution.py:25
  336.1 9.0 %collective-permute-start.14 = (f32[3,34,34,1]{2,3,1,0:T(1,128)}, f32[3,34,34,1]{2,3,1,0:T(1,128)}, u32[]{:S(2)}, u32[]{:S(2)}) collective-permute-start(f32[3,34,34,1]{2,3,1,0:T(1,128)} %copy.70), channel_id=1, source_target_pairs={{1,0},{2,1},{3,2},{4,3},{5,4},{6,5},{7,6},{9,8},{10,9},{11,10},{12... | collective-permute-start | bytes 41624 | tf_op jit(solution)/shard_map/ppermute | solution.py:28
  441.7 5.6 collective-permute-start.18
  443.0 5.8 collective-permute-start.17
  456.4 11.3 %collective-permute-start.20 = (f32[3,34,34,1]{2,1,3,0:T(8,128)}, f32[3,34,34,1]{2,1,3,0:T(8,128)S(1)}, u32[]{:S(2)}, u32[]{:S(2)}) collective-permute-start(f32[3,34,34,1]{2,1,3,0:T(8,128)} %copy.80), channel_id=1, source_target_pairs={{1,0},{2,1},{3,2},{4,3},{5,4},{6,5},{7,6},{9,8},{10,9},{11,10},{12... | collective-permute-start | bytes 41624 | tf_op jit(solution)/shard_map/ppermute | solution.py:28
  486.3 6.1 collective-permute-start.22
  487.7 11.0 %collective-permute-start.33 = (f32[3,1,32,256]{3,2,1,0:T(8,128)S(1)}, f32[3,1,32,256]{3,2,1,0:T(8,128)S(1)}, u32[]{:S(2)}, u32[]{:S(2)}) collective-permute-start(f32[3,1,32,256]{3,2,1,0:T(8,128)S(1)} %slice.782), channel_id=1, source_target_pairs={{32,0},{64,32},{96,64},{33,1},{65,33},{97,65},{34,2},{66,34},{98,6... | collective-permute-start | bytes 294920 | tf_op jit(solution)/shard_map/ppermute | solution.py:17
  492.6 11.8 %collective-permute-start.24 = (f32[3,34,1,256]{3,1,2,0:T(8,128)S(1)}, f32[3,34,1,256]{3,1,2,0:T(8,128)S(1)}, u32[]{:S(2)}, u32[]{:S(2)}) collective-permute-start(f32[3,34,1,256]{3,1,2,0:T(8,128)S(1)} %copy.84), channel_id=1, source_target_pairs={{8,0},{16,8},{24,16},{9,1},{17,9},{25,17},{10,2},{18,10},{26,18},{... | collective-permute-start | bytes 313352 | tf_op jit(solution)/shard_map/ppermute | solution.py:28
  493.9 10.7 %collective-permute-start.23 = (f32[3,34,1,256]{3,1,2,0:T(8,128)S(1)}, f32[3,34,1,256]{3,1,2,0:T(8,128)S(1)}, u32[]{:S(2)}, u32[]{:S(2)}) collective-permute-start(f32[3,34,1,256]{3,1,2,0:T(8,128)S(1)} %copy.82), channel_id=1, source_target_pairs={{0,8},{8,16},{16,24},{1,9},{9,17},{17,25},{2,10},{10,18},{18,26},{... | collective-permute-start | bytes 313352 | tf_op jit(solution)/shard_map/ppermute | solution.py:25
  498.7 5.6 collective-permute-start.34
  513.1 23.8 %collective-permute-start.26 = (f32[3,34,34,1]{2,1,3,0:T(8,128)S(1)}, f32[3,34,34,1]{2,1,3,0:T(8,128)S(1)}, u32[]{:S(2)}, u32[]{:S(2)}) collective-permute-start(f32[3,34,34,1]{2,1,3,0:T(8,128)S(1)} %copy.90), channel_id=1, source_target_pairs={{1,0},{2,1},{3,2},{4,3},{5,4},{6,5},{7,6},{9,8},{10,9},{11,10},{12... | collective-permute-start | bytes 41624 | tf_op jit(solution)/shard_map/ppermute | solution.py:28
  517.6 17.1 %collective-permute-start.25 = (f32[3,34,34,1]{2,1,3,0:T(8,128)S(1)}, f32[3,34,34,1]{2,1,3,0:T(8,128)S(1)}, u32[]{:S(2)}, u32[]{:S(2)}) collective-permute-start(f32[3,34,34,1]{2,1,3,0:T(8,128)S(1)} %copy.88), channel_id=1, source_target_pairs={{0,1},{1,2},{2,3},{3,4},{4,5},{5,6},{6,7},{8,9},{9,10},{10,11},{11... | collective-permute-start | bytes 41624 | tf_op jit(solution)/shard_map/ppermute | solution.py:25
  527.0 5.5 collective-permute-start.35
  554.0 8.9 %collective-permute-start.27 = (f32[3,1,32,256]{3,2,1,0:T(8,128)S(1)}, f32[3,1,32,256]{3,2,1,0:T(8,128)S(1)}, u32[]{:S(2)}, u32[]{:S(2)}) collective-permute-start(f32[3,1,32,256]{3,2,1,0:T(8,128)S(1)} %get-tuple-element.62), channel_id=1, source_target_pairs={{0,32},{32,64},{64,96},{1,33},{33,65},{65,97},{2,34},{34,66},{66,9... | collective-permute-start | bytes 294920 | tf_op jit(solution)/shard_map/ppermute | solution.py:25
  556.9 6.0 collective-permute-start.28
  563.2 8.4 %collective-permute-start.30 = (f32[3,34,1,256]{3,1,2,0:T(8,128)S(1)}, f32[3,34,1,256]{3,1,2,0:T(8,128)S(1)}, u32[]{:S(2)}, u32[]{:S(2)}) collective-permute-start(f32[3,34,1,256]{3,1,2,0:T(8,128)S(1)} %copy.94), channel_id=1, source_target_pairs={{8,0},{16,8},{24,16},{9,1},{17,9},{25,17},{10,2},{18,10},{26,18},{... | collective-permute-start | bytes 313352 | tf_op jit(solution)/shard_map/ppermute | solution.py:28
  564.5 7.2 %collective-permute-start.29 = (f32[3,34,1,256]{3,1,2,0:T(8,128)S(1)}, f32[3,34,1,256]{3,1,2,0:T(8,128)S(1)}, u32[]{:S(2)}, u32[]{:S(2)}) collective-permute-start(f32[3,34,1,256]{3,1,2,0:T(8,128)S(1)} %copy.92), channel_id=1, source_target_pairs={{0,8},{8,16},{16,24},{1,9},{9,17},{17,25},{2,10},{10,18},{18,26},{... | collective-permute-start | bytes 313352 | tf_op jit(solution)/shard_map/ppermute | solution.py:25
  581.5 28.7 %collective-permute-start.32 = (f32[3,34,34,1]{2,1,3,0:T(8,128)}, f32[3,34,34,1]{2,1,3,0:T(8,128)}, u32[]{:S(2)}, u32[]{:S(2)}) collective-permute-start(f32[3,34,34,1]{2,1,3,0:T(8,128)} %copy.100), channel_id=1, source_target_pairs={{1,0},{2,1},{3,2},{4,3},{5,4},{6,5},{7,6},{9,8},{10,9},{11,10},{12... | collective-permute-start | bytes 41624 | tf_op jit(solution)/shard_map/ppermute | solution.py:28
  583.4 23.8 %collective-permute-start.31 = (f32[3,34,34,1]{2,1,3,0:T(8,128)}, f32[3,34,34,1]{2,1,3,0:T(8,128)}, u32[]{:S(2)}, u32[]{:S(2)}) collective-permute-start(f32[3,34,34,1]{2,1,3,0:T(8,128)} %copy.98), channel_id=1, source_target_pairs={{0,1},{1,2},{2,3},{3,4},{4,5},{5,6},{6,7},{8,9},{9,10},{10,11},{11... | collective-permute-start | bytes 41624 | tf_op jit(solution)/shard_map/ppermute | solution.py:25
  629.6 7.9 %collective-permute-start.36 = (f32[5,1,32,256]{3,2,1,0:T(8,128)S(1)}, f32[5,1,32,256]{3,2,1,0:T(8,128)S(1)}, u32[]{:S(2)}, u32[]{:S(2)}) collective-permute-start(f32[5,1,32,256]{3,2,1,0:T(8,128)S(1)} %get-tuple-element.40), channel_id=1, source_target_pairs={{0,32},{32,64},{64,96},{1,33},{33,65},{65,97},{2,34},{34,66},{66,9... | collective-permute-start | bytes 491528 | tf_op jit(solution)/shard_map/ppermute | solution.py:25
  633.6 8.0 %collective-permute-start.37 = (f32[5,1,32,256]{3,2,1,0:T(8,128)S(1)}, f32[5,1,32,256]{3,2,1,0:T(8,128)S(1)}, u32[]{:S(2)}, u32[]{:S(2)}) collective-permute-start(f32[5,1,32,256]{3,2,1,0:T(8,128)S(1)} %get-tuple-element.41), channel_id=1, source_target_pairs={{32,0},{64,32},{96,64},{33,1},{65,33},{97,65},{34,2},{66,34},{98,6... | collective-permute-start | bytes 491528 | tf_op jit(solution)/shard_map/ppermute | solution.py:28
  641.9 6.8 collective-permute-start.38
  645.3 7.2 %collective-permute-start.39 = (f32[5,34,1,256]{3,2,1,0:T(1,128)S(1)}, f32[5,34,1,256]{3,2,1,0:T(1,128)S(1)}, u32[]{:S(2)}, u32[]{:S(2)}) collective-permute-start(f32[5,34,1,256]{3,2,1,0:T(1,128)S(1)} %get-tuple-element.39), channel_id=1, source_target_pairs={{8,0},{16,8},{24,16},{9,1},{17,9},{25,17},{10,2},{18,10},{26,18},{... | collective-permute-start | bytes 522248 | tf_op jit(solution)/shard_map/ppermute | solution.py:28
  661.4 10.9 %collective-permute-start.41 = (f32[5,34,34,1]{2,3,1,0:T(1,128)}, f32[5,34,34,1]{2,3,1,0:T(1,128)}, u32[]{:S(2)}, u32[]{:S(2)}) collective-permute-start(f32[5,34,34,1]{2,3,1,0:T(1,128)} %copy.107), channel_id=1, source_target_pairs={{1,0},{2,1},{3,2},{4,3},{5,4},{6,5},{7,6},{9,8},{10,9},{11,10},{12... | collective-permute-start | bytes 69368 | tf_op jit(solution)/shard_map/ppermute | solution.py:28
  668.3 7.5 %collective-permute-start.40 = (f32[5,34,34,1]{2,3,1,0:T(1,128)}, f32[5,34,34,1]{2,3,1,0:T(1,128)}, u32[]{:S(2)}, u32[]{:S(2)}) collective-permute-start(f32[5,34,34,1]{2,3,1,0:T(1,128)} %copy.106), channel_id=1, source_target_pairs={{0,1},{1,2},{2,3},{3,4},{4,5},{5,6},{6,7},{8,9},{9,10},{10,11},{11... | collective-permute-start | bytes 69368 | tf_op jit(solution)/shard_map/ppermute | solution.py:25
  (35 other events, 452.6 us)
